TPU v7x, 128 devices: a whole 4x4x4 slice. The times are simulated.
128 devices in a mesh: seq: 16 (over y, z), store: 8 (over x, core).
Axes of the slice: x: 4, y: 4, z: 4, core: 2. Of those that a mesh axis runs over, the one named last changes fastest.
Arguments:
- hidden: bfloat16 [16384, 4096], P('seq'), may hold values from -6 to 6
- nbr_table: bfloat16 [64, 128, 896], P('store'), may hold values from -6 to 6
- nbr_ids: int32 [256, 2], P('seq'), may hold values from 0 to 63, as said below
- w_query: bfloat16 [4096, 4096], P(None, 'store'), may hold values from -0.09375 to 0.09375
- w_key: bfloat16 [896, 4096], P(None, 'store'), may hold values from -0.1875 to 0.1875
- w_value: bfloat16 [896, 4096], P(None, 'store'), may hold values from -0.1875 to 0.1875
- w_out: bfloat16 [4096, 4096], P('store'), may hold values from -0.125 to 0.125
- enc_query: bfloat16 [896, 896], replicated, may hold values from -0.1875 to 0.1875
- enc_key: bfloat16 [4096, 896], P('seq'), may hold values from -0.09375 to 0.09375
- enc_value: bfloat16 [4096, 896], P('seq'), may hold values from -0.09375 to 0.09375
- enc_out: bfloat16 [896, 896], replicated, may hold values from -0.1875 to 0.1875
Outputs:
- cross_out: bfloat16 [16384, 4096], P('seq', 'store')
Inputs may be any that keep to these rules, and one draw needn't show every extreme that they name: `nbr_ids`: among the spans of one index of seq (16 consecutive spans), the ids fall in each owner's range k * 8 to k * 8 + 7 exactly 4 times.
All inputs are finite; a program needn't handle non-finite values.
Results may differ from a plain program's by a relative error of at most 0.03.
Values may be sent and summed in bfloat16 or wider, within the bound.
No kernel may reach another device: no remote copies, remote signals or barrier semaphores. Data moves between devices by JAX's collectives and lax.ppermute only.
A program may use at most 128 MiB of HBM per device.

v0:
```python
import math
import jax
import jax.numpy as jnp
from jax import lax
from jax.sharding import PartitionSpec as P

D = 4096
HD = 128
E = 896
EHEADS = 14
EHD = 64
CH = 64
NLEN = 128
KNB = 2
EPSILON = 1e-06


def shifted(block, axis, distance):
    devices = range(lax.axis_size(axis))
    route = [(i - distance, i) for i in devices if i - distance in devices]
    return lax.ppermute(block, axis, route)


def encoder_block(sources, cond_keys, cond_values, enc_query, enc_out):
    count = sources.shape[0]
    source_f = sources.astype(jnp.float32)
    normed = (
        source_f * lax.rsqrt(jnp.mean(source_f * source_f, axis=-1, keepdims=True) + EPSILON)
    ).astype(jnp.bfloat16)
    queries = jnp.dot(
        normed.reshape(count * NLEN, E), enc_query, preferred_element_type=jnp.float32
    ).astype(jnp.bfloat16)
    queries = queries.reshape(count, NLEN, EHEADS, EHD)
    key_heads = cond_keys.reshape(count, CH, EHEADS, EHD)
    value_heads = cond_values.reshape(count, CH, EHEADS, EHD)
    scores = jnp.einsum(
        "nqhd,nkhd->nhqk", queries, key_heads, preferred_element_type=jnp.float32
    ) / math.sqrt(EHD)
    weights = jax.nn.softmax(scores, axis=-1).astype(jnp.bfloat16)
    mixed_heads = jnp.einsum(
        "nhqk,nkhd->nqhd", weights, value_heads, preferred_element_type=jnp.float32
    ).astype(jnp.bfloat16)
    branch = jnp.dot(
        mixed_heads.reshape(count * NLEN, E), enc_out, preferred_element_type=jnp.float32
    )
    return (source_f + branch.reshape(count, NLEN, E)).astype(jnp.bfloat16)


def body(
    hidden,
    nbr_table,
    nbr_ids,
    w_query,
    w_key,
    w_value,
    w_out,
    enc_query,
    enc_key,
    enc_value,
    enc_out,
):
    store_count = lax.axis_size("store")
    store_rank = lax.axis_index("store")
    span_count = nbr_ids.shape[0]
    row_requests = span_count * KNB
    per_owner = row_requests // store_count
    blocks_here = nbr_table.shape[0]
    token_count = hidden.shape[0]
    flat_ids = nbr_ids.reshape(-1)
    owners = flat_ids // blocks_here
    slot_index = jnp.arange(row_requests, dtype=jnp.int32)
    by_owner = jnp.sort(owners * row_requests + slot_index) % row_requests
    picked = lax.dynamic_slice_in_dim(by_owner, store_rank * per_owner, per_owner)
    sources = nbr_table[flat_ids[picked] % blocks_here]
    span_of = picked // KNB
    by_span = hidden.reshape(span_count, CH, D)
    condition = by_span[span_of].reshape(per_owner * CH, D)
    shard_rows = (
        lax.all_gather(enc_key, "seq", axis=0, tiled=True),
        lax.all_gather(enc_value, "seq", axis=0, tiled=True),
    )
    key_sum = jnp.dot(condition, shard_rows[0], preferred_element_type=jnp.float32)
    value_sum = jnp.dot(condition, shard_rows[1], preferred_element_type=jnp.float32)
    cond_keys = key_sum.astype(jnp.bfloat16).reshape(per_owner, CH, E)
    cond_values = value_sum.astype(jnp.bfloat16).reshape(per_owner, CH, E)
    encoded = encoder_block(sources, cond_keys, cond_values, enc_query, enc_out)
    head_width = w_query.shape[1]
    shard_rows = lax.all_gather(encoded, "store", axis=0, tiled=True)
    flat_rows = shard_rows.reshape(-1, E)
    keys_part = jnp.dot(flat_rows, w_key, preferred_element_type=jnp.float32).astype(jnp.bfloat16)
    values_part = jnp.dot(flat_rows, w_value, preferred_element_type=jnp.float32).astype(
        jnp.bfloat16
    )
    joined = jnp.concatenate([keys_part, values_part], axis=1)
    owner_order = joined.reshape(shard_rows.shape[0], NLEN, 2 * head_width)
    key_value = owner_order[jnp.argsort(by_owner)].reshape(span_count, KNB * NLEN, 2 * head_width)
    carried = shifted(key_value[span_count - 1], "seq", 1)
    previous = jnp.concatenate([carried[None], key_value[: span_count - 1]], axis=0)
    local_heads = head_width // HD
    queries = jnp.dot(hidden, w_query, preferred_element_type=jnp.float32).astype(jnp.bfloat16)
    queries = queries.reshape(span_count, CH, local_heads, HD)
    key_heads = previous[:, :, :head_width].reshape(span_count, KNB * NLEN, local_heads, HD)
    value_heads = previous[:, :, head_width:].reshape(span_count, KNB * NLEN, local_heads, HD)
    scores = jnp.einsum(
        "cqhd,ckhd->chqk", queries, key_heads, preferred_element_type=jnp.float32
    ) / math.sqrt(HD)
    weights = jax.nn.softmax(scores, axis=-1).astype(jnp.bfloat16)
    attended = jnp.einsum(
        "chqk,ckhd->cqhd", weights, value_heads, preferred_element_type=jnp.float32
    )
    attended = attended.astype(jnp.bfloat16).reshape(token_count, head_width)
    head_terms = jnp.dot(attended, w_out, preferred_element_type=jnp.float32)
    return lax.psum_scatter(
        head_terms.astype(jnp.bfloat16), "store", scatter_dimension=1, tiled=True
    )


def solution(mesh):
    in_specs = (
        P("seq", None),
        P("store", None, None),
        P("seq", None),
        P(None, "store"),
        P(None, "store"),
        P(None, "store"),
        P("store", None),
        P(),
        P("seq", None),
        P("seq", None),
        P(),
    )
    out_specs = P("seq", "store")
    return jax.shard_map(body, mesh=mesh, in_specs=in_specs, out_specs=out_specs, check_vma=False)
```

profile of v0, /device:TPU:1, one launch (start us, length us, event | category | flops | bytes accessed | tf_op | source)
XLA Modules:
  0.0 372.8 jit_solution(12636594940149134104)
XLA Ops:
  6.5 0.0 copy-start
  6.5 0.0 all-gather.6.cloned.1.call-start
  6.5 0.7 all-gather.6.cloned.1.call-update
  7.3 0.0 all-gather.4.cloned.1.call-start
  7.3 0.7 all-gather.4.cloned.1.call-update
  8.0 0.0 all-gather.8.cloned.1.call-start
  8.1 0.8 copy.34
  8.8 0.1 reshape.108
  8.9 1.6 sort.32
  10.5 0.1 compare_select_fusion.10
  10.6 0.6 gather_fusion
  11.3 0.0 copy-done
  11.3 0.7 gather_fusion.1
  12.0 0.3 multiply_reduce_fusion.1
  12.3 0.2 fusion.10
  12.5 2.6 convolution_convert_fusion.4
  15.1 2.4 reshape.156
  17.6 5.4 %gather_fusion.2 = bf16[4,64,4096]{2,1,0:T(8,128)(2,1)} fusion(bf16[16,64,4096]{2,1,0:T(8,128)(2,1)} %bitcast.59, s32[1024]{0:T(1024)S(1)} %get-tuple-element.14), kind=kCustom, calls=%fused_computation.2 | custom fusion | bytes 4194320 | tf_op jit(solution)/shard_map/gather | solution.py:77
  23.0 56.1 %all-gather.6.cloned.1.call-done = bf16[4096,896]{1,0:T(8,128)(2,1)} async-done(((bf16[256,896]{1,0:T(8,128)(2,1)}), bf16[4096,896]{1,0:T(8,128)(2,1)}) %all-gather.6.cloned.1.call-update) | async-done | bytes 7340048 | tf_op jit(solution)/shard_map/all_gather | solution.py:79
  79.1 6.1 %convolution_convert_fusion.6 = bf16[256,896]{1,0:T(8,128)(2,1)S(1)} fusion(bf16[256,4096]{1,0:T(8,128)(2,1)} %bitcast.54, bf16[4096,896]{1,0:T(8,128)(2,1)} %all-gather.6.cloned.1.call-done), kind=kOutput, calls=%fused_computation.37 | convolution fusion | flops 1879277568 | bytes 9895936 | tf_op jit(solution)/shard_map/dot_general | solution.py:82
  85.1 0.7 reshape.157
  85.8 2.9 fusion.8
  88.7 0.0 copy-start.3
  88.7 1.3 copy-done.3
  90.0 0.5 fusion.45
  90.5 56.6 %all-gather.4.cloned.1.call-done = bf16[4096,896]{1,0:T(8,128)(2,1)} async-done(((bf16[256,896]{1,0:T(8,128)(2,1)}), bf16[4096,896]{1,0:T(8,128)(2,1)}) %all-gather.4.cloned.1.call-update) | async-done | bytes 7340048 | tf_op jit(solution)/shard_map/all_gather | solution.py:80
  147.1 6.1 %convolution_convert_fusion.7 = bf16[256,896]{1,0:T(8,128)(2,1)S(1)} fusion(bf16[256,4096]{1,0:T(8,128)(2,1)} %bitcast.55, bf16[4096,896]{1,0:T(8,128)(2,1)} %all-gather.4.cloned.1.call-done), kind=kOutput, calls=%fused_computation.38 | convolution fusion | flops 1879277568 | bytes 9895936 | tf_op jit(solution)/shard_map/dot_general | solution.py:83
  153.2 1.7 reshape.155
  154.8 0.0 copy-start.4
  154.8 3.7 convolution_convert_fusion.5
  158.6 0.0 copy-done.4
  158.6 3.4 add_convert_fusion
  161.9 0.0 all-gather.8.cloned.1.call-update
  161.9 0.2 reduce-scatter.2.cloned.1.call-start
  162.2 1.7 sort.33
  163.9 43.5 %all-gather.8.cloned.1.call-done = bf16[32,128,896]{2,1,0:T(8,128)(2,1)} async-done(((bf16[4,128,896]{2,1,0:T(8,128)(2,1)}), bf16[32,128,896]{2,1,0:T(8,128)(2,1)}) %all-gather.8.cloned.1.call-update) | async-done | bytes 7340048 | tf_op jit(solution)/shard_map/all_gather | solution.py:88
  207.4 0.0 copy-start.5
  207.4 9.9 %convolution_convert_fusion.1 = bf16[4096,512]{0,1:T(8,128)(2,1)} fusion(bf16[4096,896]{1,0:T(8,128)(2,1)} %bitcast.60, bf16[896,512]{1,0:T(8,128)(2,1)} %param.16), kind=kOutput, calls=%fused_computation.10 | convolution fusion | flops 3760193536 | bytes 12451840 | tf_op jit(solution)/shard_map/dot_general | solution.py:91
  217.4 0.0 copy-done.5
  217.4 0.0 copy-done.6
  217.4 6.3 %convolution_convert_fusion.2 = bf16[4096,512]{0,1:T(8,128)(2,1)} fusion(bf16[4096,896]{1,0:T(8,128)(2,1)S(1)} %bitcast.61, bf16[896,512]{1,0:T(8,128)(2,1)S(1)} %copy-done.6), kind=kOutput, calls=%fused_computation.11 | convolution fusion | flops 3760193536 | bytes 12451840 | tf_op jit(solution)/shard_map/dot_general | solution.py:90
  223.6 7.8 %pad_maximum_fusion = bf16[4096,1024]{0,1:T(8,128)(2,1)} fusion(bf16[4096,512]{0,1:T(8,128)(2,1)} %convolution_convert_fusion.1, bf16[4096,512]{0,1:T(8,128)(2,1)} %convolution_convert_fusion.2), kind=kLoop, calls=%fused_computation.6 | loop fusion | flops 16777216 | bytes 16777216 | tf_op jit(solution)/shard_map/concatenate | solution.py:94
  231.4 11.9 %copy.58 = bf16[4096,1024]{1,0:T(8,128)(2,1)} copy(bf16[4096,1024]{0,1:T(8,128)(2,1)} %pad_maximum_fusion) | data formatting | bytes 16777216 | tf_op jit(solution)/shard_map/reshape | solution.py:95
  243.3 8.4 %gather_fusion.3 = bf16[32,128,1024]{2,1,0:T(8,128)(2,1)} fusion(bf16[32,128,1024]{2,1,0:T(8,128)(2,1)} %bitcast.51, s32[1024]{0:T(1024)S(1)} %pad_clamp_fusion), kind=kCustom, calls=%fused_computation.3 | custom fusion | bytes 16777344 | tf_op jit(solution)/shard_map/gather | solution.py:96
  251.7 1.9 slice.29
  253.6 3.2 collective-permute-start
  256.8 9.1 %convolution_convert_fusion.3 = bf16[1024,512]{1,0:T(8,128)(2,1)S(1)} fusion(bf16[1024,4096]{1,0:T(8,128)(2,1)} %param.11, bf16[4096,512]{1,0:T(8,128)(2,1)} %param.14), kind=kOutput, calls=%fused_computation.33 | convolution fusion | flops 4295491584 | bytes 13631488 | tf_op jit(solution)/shard_map/dot_general | solution.py:100
  265.9 0.5 reshape.115
  266.4 0.0 slice-start
  266.4 1.8 collective-permute-done
  268.1 1.5 slice-done
  269.6 3.7 pad_maximum_fusion.1
  273.3 6.4 %copy.44 = bf16[16,256,512]{1,2,0:T(8,128)(2,1)} copy(bf16[16,256,512]{2,1,0:T(8,128)(2,1)} %get-tuple-element.10) | data formatting | bytes 8388608 | tf_op jit(solution)/shard_map/slice | solution.py:102
  279.7 2.9 fusion.20
  282.6 0.0 copy-start.2
  282.6 2.0 copy-done.2
  284.6 1.6 fusion.46
  286.1 6.4 %copy.43 = bf16[16,256,512]{1,2,0:T(8,128)(2,1)} copy(bf16[16,256,512]{2,1,0:T(8,128)(2,1)} %get-tuple-element.11) | data formatting | bytes 8388608 | tf_op jit(solution)/shard_map/slice | solution.py:103
  292.5 11.9 %fusion.17 = bf16[16,64,4,128]{3,1,2,0:T(8,128)(2,1)S(1)} fusion(bf16[16,256,4,128]{1,3,2,0:T(8,128)(2,1)} %bitcast.53, f32[16,4,64]{2,1,0:T(4,128)S(1)} %fusion.46, f32[16,4,64,256]{3,2,1,0:T(8,128)} %copy-done.2), kind=kOutput, calls=%fused_computation.36 | convolution fusion | flops 274206976 | bytes 9453568 | tf_op jit(solution)/shard_map/chqk,ckhd->cqhd/dot_general | solution.py:108
  304.5 0.9 copy.48
  305.4 8.9 %convolution_convert_fusion = bf16[1024,4096]{1,0:T(8,128)(2,1)} fusion(bf16[512,4096]{1,0:T(8,128)(2,1)} %param.17, bf16[128,8,4,128]{3,2,1,0:T(4,128)(2,1)S(1)} %bitcast.56), kind=kOutput, calls=%fused_computation.9 | convolution fusion | flops 4299161600 | bytes 13631488 | tf_op jit(solution)/shard_map/dot_general | solution.py:112
  314.3 0.0 reduce-scatter.2.cloned.1.call-update
  314.3 51.9 %reduce-scatter.2.cloned.1.call-done = bf16[1024,512]{1,0:T(8,128)(2,1)} async-done(((bf16[1024,4096]{1,0:T(8,128)(2,1)}), bf16[1024,512]{1,0:T(8,128)(2,1)}) %reduce-scatter.2.cloned.1.call-update) | async-done | bytes 1048592 | tf_op jit(solution)/shard_map/reduce_scatter | solution.py:113
  366.2 0.0 copy-done.1
  (12 shorter events, 0.1 us)
Async XLA Ops:
  6.5 4.8 %copy-start = (bf16[8,128,896]{2,1,0:T(8,128)(2,1)S(1)}, bf16[8,128,896]{2,1,0:T(8,128)(2,1)}, u32[]{:S(2)}) copy-start(bf16[8,128,896]{2,1,0:T(8,128)(2,1)} %param.12) | copy-start | bytes 5505028
  6.5 72.5 %all-gather.6.cloned.1.call-start = ((), (), s32[]{:S(2)}) async-start(), calls=%async_computation.2 | async-start | bytes 7798784 | tf_op jit(solution)/shard_map/all_gather | solution.py:79
  7.3 139.9 %all-gather.4.cloned.1.call-start = ((), (), s32[]{:S(2)}) async-start(), calls=%async_computation.1 | async-start | bytes 7798784 | tf_op jit(solution)/shard_map/all_gather | solution.py:80
  8.0 199.4 %all-gather.8.cloned.1.call-start = ((), (), s32[]{:S(2)}) async-start(), calls=%async_computation.3 | async-start | bytes 8257536 | tf_op jit(solution)/shard_map/all_gather | solution.py:88
  88.7 1.3 copy-start.3
  154.8 3.7 copy-start.4
  161.9 204.3 %reduce-scatter.2.cloned.1.call-start = ((), (), s32[]{:S(2)}) async-start(), calls=%async_computation.4 | async-start | bytes 9437184 | tf_op jit(solution)/shard_map/reduce_scatter | solution.py:113
  207.4 10.0 %copy-start.5 = (bf16[32,128,896]{2,1,0:T(8,128)(2,1)S(1)}, bf16[32,128,896]{2,1,0:T(8,128)(2,1)}, u32[]{:S(2)}) copy-start(bf16[32,128,896]{2,1,0:T(8,128)(2,1)} %all-gather.8.cloned.1.call-done) | copy-start | bytes 22020100
  207.4 10.0 %copy-start.6 = (bf16[896,512]{1,0:T(8,128)(2,1)S(1)}, bf16[896,512]{1,0:T(8,128)(2,1)}, u32[]{:S(2)}) copy-start(bf16[896,512]{1,0:T(8,128)(2,1)} %param.15) | copy-start | bytes 2752516
  253.6 14.5 %collective-permute-start = (bf16[256,1024]{1,0:T(8,128)(2,1)}, bf16[256,1024]{1,0:T(8,128)(2,1)S(1)}, u32[]{:S(2)}, u32[]{:S(2)}) collective-permute-start(bf16[256,1024]{1,0:T(8,128)(2,1)} %bitcast.11), channel_id=1, source_target_pairs={{0,8},{8,16},{16,24},{24,32},{32,40},{40,48},{48,56},{56,64},{64,7... | collective-permute-start | bytes 1572872 | tf_op jit(solution)/shard_map/ppermute | solution.py:21
  266.4 3.2 slice-start
  282.6 2.0 copy-start.2
  314.3 51.9 %copy-start.1 = (bf16[8,128,896]{2,1,0:T(8,128)(2,1)S(1)}, bf16[8,128,896]{2,1,0:T(8,128)(2,1)}, u32[]{:S(2)}) copy-start(bf16[8,128,896]{2,1,0:T(8,128)(2,1)} %param.12) | copy-start | bytes 5505028
Sparse Core Ops, SparseCore 0:
  9.5 69.4 all-gather.5
  81.2 65.8 all-gather.3
  162.1 45.3 all-gather.7
  314.5 51.7 reduce-scatter.1
where the time goes:
time: 374 us; the launch traced here: 373 us
  waiting for transfers between devices  211 us (56%)
  matrix products  73.7 us (20%)
  local copies, waits for them, and re-layouts  53.5 us (14%)
  other arithmetic  17.5 us (5%)
  between operations  13.3 us (4%)
    all_gather x1, waiting for transfers between devices, body(): lax.all_gather(enc_value, 'seq', axis=0, tiled=True)  56.6 us
    all_gather x1, waiting for transfers between devices, body(): lax.all_gather(enc_key, 'seq', axis=0, tiled=True)  56.1 us
    reduce_scatter x1, waiting for transfers between devices, body(): lax.psum_scatter(head_terms.astype(jnp.bfloat16), 'store', scatter_dimens...  51.9 us
    all_gather x1, waiting for transfers between devices, body(): shard_rows = lax.all_gather(encoded, 'store', axis=0, tiled=True)  43.5 us
    dot_general x1, matrix products, body(): jnp.einsum('chqk,ckhd->cqhd', weights, value_heads, preferred_element_typ...  11.9 us
    reshape x1, local copies, waits for them, and re-layouts, body(): owner_order = joined.reshape(shard_rows.shape[0], NLEN, 2 * head_width)  11.9 us
    dot_general x1, matrix products, body(): jnp.dot(flat_rows, w_value, preferred_element_type=jnp.float32)  9.94 us
    dot_general x1, matrix products, body(): jnp.dot(hidden, w_query, preferred_element_type=jnp.float32)  9.05 us
  transfers between devices with their start and end apart: 5, of which 5 were waited for; matrix products, arithmetic and copies ran while one was open for 10% of the time, Pallas kernels for 0%

commit v1 on v0

--- a/solution.py
+++ b/solution.py
@@ -85,7 +85,19 @@
     cond_values = value_sum.astype(jnp.bfloat16).reshape(per_owner, CH, E)
     encoded = encoder_block(sources, cond_keys, cond_values, enc_query, enc_out)
     head_width = w_query.shape[1]
-    shard_rows = lax.all_gather(encoded, "store", axis=0, tiled=True)
+
+    def serve_the_modes(original, bus_axis):
+        return jnp.concatenate(
+            lax.all_to_all(
+                jnp.stack([original] * lax.axis_size(bus_axis)),
+                axis_name=bus_axis,
+                split_axis=0,
+                concat_axis=0,
+            ),
+            axis=0,
+        )
+
+    shard_rows = serve_the_modes(encoded, "store")
     flat_rows = shard_rows.reshape(-1, E)
     keys_part = jnp.dot(flat_rows, w_key, preferred_element_type=jnp.float32).astype(jnp.bfloat16)
     values_part = jnp.dot(flat_rows, w_value, preferred_element_type=jnp.float32).astype(

time: 374 us -> 420 us (1.12)
  waiting for transfers between devices: 211 us -> 247 us
  starting transfers between devices: 3.49 us -> 8.56 us
    all_to_all x0 -> x1, waiting for transfers between devices: none -> 81 us  [serve_the_modes(): lax.all_to_all(jnp.stack([original] * lax.axis_size(bus_axis)), axis_name...]
    all_gather x1 -> x0, waiting for transfers between devices: 43.5 us -> none  [body(): shard_rows = lax.all_gather(encoded, 'store', axis=0, tiled=True)]
    all_to_all x0 -> x1, starting transfers between devices: none -> 5.53 us  [serve_the_modes(): lax.all_to_all(jnp.stack([original] * lax.axis_size(bus_axis)), axis_name...]
  transfers between devices with their start and end apart: 5 -> 5, of which waited for: 5 -> 5; matrix products, arithmetic and copies ran while one was open for 10% -> 9% of each run, Pallas kernels for 0% -> 0%
where the time goes in v1:
time: 420 us; the launch traced here: 419 us
  waiting for transfers between devices  247 us (59%)
  matrix products  75.1 us (18%)
  local copies, waits for them, and re-layouts  57.3 us (14%)
  other arithmetic  17.4 us (4%)
  between operations  13.3 us (3%)
  starting transfers between devices  8.56 us (2%)
    all_to_all x1, waiting for transfers between devices, serve_the_modes(): lax.all_to_all(jnp.stack([original] * lax.axis_size(bus_axis)), axis_name...  81 us
    all_gather x1, waiting for transfers between devices, body(): lax.all_gather(enc_value, 'seq', axis=0, tiled=True)  56.6 us
    all_gather x1, waiting for transfers between devices, body(): lax.all_gather(enc_key, 'seq', axis=0, tiled=True)  56.1 us
    reduce_scatter x1, waiting for transfers between devices, body(): lax.psum_scatter(head_terms.astype(jnp.bfloat16), 'store', scatter_dimens...  51.3 us
    dot_general x1, matrix products, body(): jnp.einsum('chqk,ckhd->cqhd', weights, value_heads, preferred_element_typ...  11.9 us
    reshape x1, local copies, waits for them, and re-layouts, body(): owner_order = joined.reshape(shard_rows.shape[0], NLEN, 2 * head_width)  11.9 us
    dot_general x1, matrix products, body(): jnp.dot(flat_rows, w_value, preferred_element_type=jnp.float32)  9.24 us
    dot_general x1, matrix products, body(): jnp.dot(flat_rows, w_key, preferred_element_type=jnp.float32)  9.21 us
  transfers between devices with their start and end apart: 5, of which 5 were waited for; matrix products, arithmetic and copies ran while one was open for 9% of the time, Pallas kernels for 0%

profile of v1, /device:TPU:1, one launch (start us, length us, event | category | flops | bytes accessed | tf_op | source)
XLA Modules:
  0.0 419.1 jit_solution(7468678962293575318)
XLA Ops:
  6.5 0.0 copy-start
  6.5 0.0 all-gather.5.cloned.1.call-start
  6.5 0.7 all-gather.5.cloned.1.call-update
  7.3 0.0 all-gather.3.cloned.1.call-start
  7.3 0.7 all-gather.3.cloned.1.call-update
  8.0 0.8 copy.19
  8.8 0.1 reshape.107
  8.9 1.6 sort.32
  10.5 0.1 compare_select_fusion.10
  10.6 0.6 gather_fusion
  11.3 0.0 copy-done
  11.3 0.7 gather_fusion.1
  12.0 0.3 multiply_reduce_fusion.1
  12.2 0.2 fusion.10
  12.5 2.6 convolution_convert_fusion.4
  15.1 2.4 reshape.154
  17.5 5.4 %gather_fusion.2 = bf16[4,64,4096]{2,1,0:T(8,128)(2,1)} fusion(bf16[16,64,4096]{2,1,0:T(8,128)(2,1)} %bitcast.59, s32[1024]{0:T(1024)S(1)} %get-tuple-element.14), kind=kCustom, calls=%fused_computation.2 | custom fusion | bytes 4194320 | tf_op jit(solution)/shard_map/gather | solution.py:77
  22.9 56.1 %all-gather.5.cloned.1.call-done = bf16[4096,896]{1,0:T(8,128)(2,1)} async-done(((bf16[256,896]{1,0:T(8,128)(2,1)}), bf16[4096,896]{1,0:T(8,128)(2,1)}) %all-gather.5.cloned.1.call-update) | async-done | bytes 7340048 | tf_op jit(solution)/shard_map/all_gather | solution.py:79
  79.1 6.1 %convolution_convert_fusion.6 = bf16[256,896]{1,0:T(8,128)(2,1)S(1)} fusion(bf16[256,4096]{1,0:T(8,128)(2,1)} %bitcast.54, bf16[4096,896]{1,0:T(8,128)(2,1)} %all-gather.5.cloned.1.call-done), kind=kOutput, calls=%fused_computation.37 | convolution fusion | flops 1879277568 | bytes 9895936 | tf_op jit(solution)/shard_map/dot_general | solution.py:82
  85.1 0.7 reshape.155
  85.8 2.9 fusion.8
  88.7 0.0 copy-start.3
  88.7 1.3 copy-done.3
  90.0 0.5 fusion.45
  90.5 56.6 %all-gather.3.cloned.1.call-done = bf16[4096,896]{1,0:T(8,128)(2,1)} async-done(((bf16[256,896]{1,0:T(8,128)(2,1)}), bf16[4096,896]{1,0:T(8,128)(2,1)}) %all-gather.3.cloned.1.call-update) | async-done | bytes 7340048 | tf_op jit(solution)/shard_map/all_gather | solution.py:80
  147.1 6.1 %convolution_convert_fusion.7 = bf16[256,896]{1,0:T(8,128)(2,1)S(1)} fusion(bf16[256,4096]{1,0:T(8,128)(2,1)} %bitcast.55, bf16[4096,896]{1,0:T(8,128)(2,1)} %all-gather.3.cloned.1.call-done), kind=kOutput, calls=%fused_computation.38 | convolution fusion | flops 1879277568 | bytes 9895936 | tf_op jit(solution)/shard_map/dot_general | solution.py:83
  153.2 0.7 reshape.153
  153.9 3.3 convolution_convert_fusion.5
  157.1 3.0 add_convert_fusion
  160.1 4.1 stack.2
  164.2 0.0 copy-start.4
  164.2 5.5 %all-to-all-start = ((bf16[8,4,128,896]{3,2,1,0:T(8,128)(2,1)}), bf16[8,4,128,896]{3,2,1,0:T(8,128)(2,1)}, u32[]{:S(2)}, u32[]{:S(2)}) async-start(bf16[8,4,128,896]{3,2,1,0:T(8,128)(2,1)} %stack.2), calls=%async_computation | async-start | bytes 14680064 | tf_op jit(solution)/shard_map/all_to_all | solution.py:91
  169.7 0.0 reduce-scatter.2.cloned.1.call-start
  169.7 1.6 sort.33
  171.3 81.0 %all-to-all-done = bf16[8,4,128,896]{3,2,1,0:T(8,128)(2,1)} async-done(((bf16[8,4,128,896]{3,2,1,0:T(8,128)(2,1)}), bf16[8,4,128,896]{3,2,1,0:T(8,128)(2,1)}, u32[]{:S(2)}, u32[]{:S(2)}) %all-to-all-start) | async-done | bytes 7340064 | tf_op jit(solution)/shard_map/all_to_all | solution.py:91
  252.3 0.0 copy-done.4
  252.3 0.0 copy-start.5
  252.3 9.2 %convolution_convert_fusion.1 = bf16[4096,512]{0,1:T(8,128)(2,1)} fusion(bf16[4096,896]{1,0:T(8,128)(2,1)} %bitcast.9, bf16[896,512]{1,0:T(8,128)(2,1)S(1)} %copy-done.4), kind=kOutput, calls=%fused_computation.10 | convolution fusion | flops 3760193536 | bytes 12451840 | tf_op jit(solution)/shard_map/dot_general | solution.py:103
  261.6 0.0 copy-done.5
  261.6 9.2 %convolution_convert_fusion.2 = bf16[4096,512]{0,1:T(8,128)(2,1)} fusion(bf16[4096,896]{1,0:T(8,128)(2,1)} %bitcast.9, bf16[896,512]{1,0:T(8,128)(2,1)S(1)} %copy-done.5), kind=kOutput, calls=%fused_computation.11 | convolution fusion | flops 3760193536 | bytes 12451840 | tf_op jit(solution)/shard_map/dot_general | solution.py:102
  270.8 7.8 %pad_maximum_fusion = bf16[4096,1024]{0,1:T(8,128)(2,1)} fusion(bf16[4096,512]{0,1:T(8,128)(2,1)} %convolution_convert_fusion.1, bf16[4096,512]{0,1:T(8,128)(2,1)} %convolution_convert_fusion.2), kind=kLoop, calls=%fused_computation.6 | loop fusion | flops 16777216 | bytes 16777216 | tf_op jit(solution)/shard_map/concatenate | solution.py:106
  278.6 11.9 %copy.43 = bf16[4096,1024]{1,0:T(8,128)(2,1)} copy(bf16[4096,1024]{0,1:T(8,128)(2,1)} %pad_maximum_fusion) | data formatting | bytes 16777216 | tf_op jit(solution)/shard_map/reshape | solution.py:107
  290.5 8.4 %gather_fusion.3 = bf16[32,128,1024]{2,1,0:T(8,128)(2,1)} fusion(bf16[32,128,1024]{2,1,0:T(8,128)(2,1)} %bitcast.51, s32[1024]{0:T(1024)S(1)} %pad_clamp_fusion), kind=kCustom, calls=%fused_computation.3 | custom fusion | bytes 16777344 | tf_op jit(solution)/shard_map/gather | solution.py:108
  298.9 1.9 slice.29
  300.8 3.0 collective-permute-start
  303.8 9.1 %convolution_convert_fusion.3 = bf16[1024,512]{1,0:T(8,128)(2,1)S(1)} fusion(bf16[1024,4096]{1,0:T(8,128)(2,1)} %param.11, bf16[4096,512]{1,0:T(8,128)(2,1)} %param.14), kind=kOutput, calls=%fused_computation.33 | convolution fusion | flops 4295491584 | bytes 13631488 | tf_op jit(solution)/shard_map/dot_general | solution.py:112
  312.8 0.5 reshape.113
  313.4 0.0 slice-start
  313.4 1.0 collective-permute-done
  314.4 2.2 slice-done
  316.6 3.7 pad_maximum_fusion.1
  320.3 6.4 %copy.29 = bf16[16,256,512]{1,2,0:T(8,128)(2,1)} copy(bf16[16,256,512]{2,1,0:T(8,128)(2,1)} %get-tuple-element.10) | data formatting | bytes 8388608 | tf_op jit(solution)/shard_map/slice | solution.py:114
  326.7 2.9 fusion.20
  329.6 0.0 copy-start.2
  329.6 2.0 copy-done.2
  331.6 1.6 fusion.46
  333.1 6.4 %copy.28 = bf16[16,256,512]{1,2,0:T(8,128)(2,1)} copy(bf16[16,256,512]{2,1,0:T(8,128)(2,1)} %get-tuple-element.11) | data formatting | bytes 8388608 | tf_op jit(solution)/shard_map/slice | solution.py:115
  339.5 11.9 %fusion.17 = bf16[16,64,4,128]{3,1,2,0:T(8,128)(2,1)S(1)} fusion(bf16[16,256,4,128]{1,3,2,0:T(8,128)(2,1)} %bitcast.53, f32[16,4,64]{2,1,0:T(4,128)S(1)} %fusion.46, f32[16,4,64,256]{3,2,1,0:T(8,128)} %copy-done.2), kind=kOutput, calls=%fused_computation.36 | convolution fusion | flops 274206976 | bytes 9453568 | tf_op jit(solution)/shard_map/chqk,ckhd->cqhd/dot_general | solution.py:120
  351.5 0.9 copy.33
  352.4 8.9 %convolution_convert_fusion = bf16[1024,4096]{1,0:T(8,128)(2,1)} fusion(bf16[512,4096]{1,0:T(8,128)(2,1)} %param.17, bf16[128,8,4,128]{3,2,1,0:T(4,128)(2,1)S(1)} %bitcast.56), kind=kOutput, calls=%fused_computation.9 | convolution fusion | flops 4299161600 | bytes 13631488 | tf_op jit(solution)/shard_map/dot_general | solution.py:124
  361.3 0.0 copy-start.1
  361.3 0.0 reduce-scatter.2.cloned.1.call-update
  361.3 51.3 %reduce-scatter.2.cloned.1.call-done = bf16[1024,512]{1,0:T(8,128)(2,1)} async-done(((bf16[1024,4096]{1,0:T(8,128)(2,1)}), bf16[1024,512]{1,0:T(8,128)(2,1)}) %reduce-scatter.2.cloned.1.call-update) | async-done | bytes 1048592 | tf_op jit(solution)/shard_map/reduce_scatter | solution.py:125
  412.6 0.0 copy-done.1
  (10 shorter events, 0.1 us)
Async XLA Ops:
  6.5 4.7 %copy-start = (bf16[8,128,896]{2,1,0:T(8,128)(2,1)S(1)}, bf16[8,128,896]{2,1,0:T(8,128)(2,1)}, u32[]{:S(2)}) copy-start(bf16[8,128,896]{2,1,0:T(8,128)(2,1)} %param.12) | copy-start | bytes 5505028
  6.5 72.5 %all-gather.5.cloned.1.call-start = ((), (), s32[]{:S(2)}) async-start(), calls=%async_computation.3 | async-start | bytes 7798784 | tf_op jit(solution)/shard_map/all_gather | solution.py:79
  7.3 139.9 %all-gather.3.cloned.1.call-start = ((), (), s32[]{:S(2)}) async-start(), calls=%async_computation.2 | async-start | bytes 7798784 | tf_op jit(solution)/shard_map/all_gather | solution.py:80
  88.7 1.3 copy-start.3
  164.2 88.2 %copy-start.4 = (bf16[896,512]{1,0:T(8,128)(2,1)S(1)}, bf16[896,512]{1,0:T(8,128)(2,1)}, u32[]{:S(2)}) copy-start(bf16[896,512]{1,0:T(8,128)(2,1)} %param.16) | copy-start | bytes 2752516
  164.2 88.2 %all-to-all-start = ((bf16[8,4,128,896]{3,2,1,0:T(8,128)(2,1)}), bf16[8,4,128,896]{3,2,1,0:T(8,128)(2,1)}, u32[]{:S(2)}, u32[]{:S(2)}) async-start(bf16[8,4,128,896]{3,2,1,0:T(8,128)(2,1)} %stack.2), calls=%async_computation | async-start | bytes 14680064 | tf_op jit(solution)/shard_map/all_to_all | solution.py:91
  169.7 242.9 %reduce-scatter.2.cloned.1.call-start = ((), (), s32[]{:S(2)}) async-start(), calls=%async_computation.4 | async-start | bytes 9437184 | tf_op jit(solution)/shard_map/reduce_scatter | solution.py:125
  252.3 9.2 %copy-start.5 = (bf16[896,512]{1,0:T(8,128)(2,1)S(1)}, bf16[896,512]{1,0:T(8,128)(2,1)}, u32[]{:S(2)}) copy-start(bf16[896,512]{1,0:T(8,128)(2,1)} %param.15) | copy-start | bytes 2752516
  300.8 13.6 %collective-permute-start = (bf16[256,1024]{1,0:T(8,128)(2,1)}, bf16[256,1024]{1,0:T(8,128)(2,1)S(1)}, u32[]{:S(2)}, u32[]{:S(2)}) collective-permute-start(bf16[256,1024]{1,0:T(8,128)(2,1)} %bitcast.11), channel_id=1, source_target_pairs={{0,8},{8,16},{16,24},{24,32},{32,40},{40,48},{48,56},{56,64},{64,7... | collective-permute-start | bytes 1572872 | tf_op jit(solution)/shard_map/ppermute | solution.py:21
  313.4 3.2 slice-start
  329.6 2.0 copy-start.2
  361.3 51.3 %copy-start.1 = (bf16[8,128,896]{2,1,0:T(8,128)(2,1)S(1)}, bf16[8,128,896]{2,1,0:T(8,128)(2,1)}, u32[]{:S(2)}) copy-start(bf16[8,128,896]{2,1,0:T(8,128)(2,1)} %param.12) | copy-start | bytes 5505028
Sparse Core Ops, SparseCore 0:
  9.5 69.4 all-gather.4
  81.2 65.8 all-gather.2
  361.4 51.0 reduce-scatter.1
